TPU v7x, 32 devices: a whole 2x2x4 slice. The times are simulated.
32 devices in a mesh: ctx: 8 (over z, y), tp: 4 (over x, core).
Axes of the slice: x: 2, y: 2, z: 4, core: 2. Of those that a mesh axis runs over, the one named last changes fastest.
Arguments:
- qkv: bfloat16 [1024, 3, 8192], P(('ctx', 'tp')), may hold values from -6 to 6
- filters: float32 [3, 7, 8192], P(None, None, 'tp'), may hold values from -1.5 to 1.5
- doc_ids: int32 [8], replicated, may hold values from 0 to 1, never falling along the last dimension, each value on 1 to 5 neighbouring positions
- upstream: bfloat16 [1024, 8192], P('ctx', 'tp'), may hold values from -6 to 6
Outputs:
- attended: bfloat16 [1024, 8192], P('ctx', 'tp')
- qkv_grad: bfloat16 [1024, 3, 8192], P(('ctx', 'tp'))
- filter_grad: float32 [3, 7, 8192], P(None, None, 'tp')
Inputs may be any that keep to these rules, and one draw needn't show every extreme that they name: doc_ids never falls along the sequence; every document covers 1 to 5 whole blocks of 128 tokens.
All inputs are finite; a program needn't handle non-finite values.
Results may differ from a plain program's by a relative error of at most 0.014.
The roundings to bfloat16 on the way count: a program that leaves them out, or rounds other values in their place, can miss the bound.
Values may be sent and summed in bfloat16 or wider, within the bound.
No kernel may reach another device: no remote copies, remote signals or barrier semaphores. Data moves between devices by JAX's collectives and lax.ppermute only.
A program may use at most 128 MiB of HBM per device.

v0:
```python
import jax
import jax.numpy as jnp
from jax import lax
from jax.sharding import PartitionSpec as P

HEAD_DIM = 128
KW = 7
BLOCK = 128
STEPS = 4


def from_behind(value, axis, steps):
    count = lax.axis_size(axis)
    first, last = (max(0, -steps), min(count, count - steps))
    return lax.ppermute(value, axis, [(source, source + steps) for source in range(first, last)])


def block_docs(doc_ids, first_block, count):
    start = jnp.maximum(first_block, 0)
    picked = lax.dynamic_slice_in_dim(doc_ids, start, count)
    return jnp.repeat(picked, BLOCK)


def shards(qkv, filters, doc_ids, upstream):
    local = lax.all_to_all(qkv, "tp", split_axis=2, concat_axis=0, tiled=True)
    tokens = local.shape[0]
    width = local.shape[2]
    heads = width // HEAD_DIM
    blocks_here = tokens // BLOCK
    logit_scale = HEAD_DIM ** (-0.5)
    position = lax.axis_index("ctx")
    reach = STEPS + 1
    rim = from_behind(local[tokens - (KW - 1) :], "ctx", 1)
    inputs = jnp.concatenate([rim, local], axis=0).astype(jnp.float32)
    mixed = sum(
        (filters[:, lag, :] * inputs[KW - 1 - lag : KW - 1 - lag + tokens] for lag in range(KW))
    )
    mixed = mixed.astype(jnp.bfloat16)
    queries = mixed[:, 0].reshape(tokens, heads, HEAD_DIM)
    key_value = mixed[:, 1:3]
    tiles = [key_value]
    current = key_value
    for distance in range(1, STEPS + 1):
        current = from_behind(current, "ctx", 1)
        tiles.append(current)
    joined = jnp.concatenate(tiles, axis=0)
    keys = joined[:, 0].reshape(reach * tokens, heads, HEAD_DIM)
    values = joined[:, 1].reshape(reach * tokens, heads, HEAD_DIM)
    rows = jnp.arange(tokens)
    query_token = position * tokens + rows
    query_doc = block_docs(doc_ids, position * blocks_here, blocks_here)
    key_tokens = jnp.concatenate(
        [(position - distance) * tokens + rows for distance in range(reach)]
    )
    key_docs = jnp.concatenate(
        [
            block_docs(doc_ids, (position - distance) * blocks_here, blocks_here)
            for distance in range(reach)
        ]
    )
    allowed = (
        (key_tokens[None, :] >= 0)
        & (key_tokens[None, :] <= query_token[:, None])
        & (key_docs[None, :] == query_doc[:, None])
    )
    raw = (
        jnp.einsum("qhd,khd->hqk", queries, keys, preferred_element_type=jnp.float32) * logit_scale
    )
    masked = jnp.where(allowed[None], raw, -1e30)
    row_max = masked.max(axis=2)
    expo = jnp.where(allowed[None], jnp.exp(masked - row_max[:, :, None]), 0.0)
    row_sum = expo.sum(axis=2)
    weighted_values = jnp.einsum(
        "hqk,khd->qhd", expo.astype(jnp.bfloat16), values, preferred_element_type=jnp.float32
    )
    attended = (weighted_values / row_sum.T[:, :, None]).astype(jnp.bfloat16)
    grad_out = upstream.reshape(tokens, heads, HEAD_DIM)
    delta = jnp.sum(grad_out.astype(jnp.float32) * attended.astype(jnp.float32), axis=-1).T
    prob = expo / row_sum[:, :, None]
    value_part = jnp.einsum(
        "hqk,qhd->khd", prob.astype(jnp.bfloat16), grad_out, preferred_element_type=jnp.float32
    )
    probability_gradient = jnp.einsum(
        "qhd,khd->hqk", grad_out, values, preferred_element_type=jnp.float32
    )
    score_gradient = (prob * (probability_gradient - delta[:, :, None]) * logit_scale).astype(
        jnp.bfloat16
    )
    query_gradient_rows = jnp.einsum(
        "hqk,khd->qhd", score_gradient, keys, preferred_element_type=jnp.float32
    )
    key_part = jnp.einsum(
        "hqk,qhd->khd", score_gradient, queries, preferred_element_type=jnp.float32
    )
    stacked = jnp.stack(
        [key_part.reshape(reach, tokens, width), value_part.reshape(reach, tokens, width)], axis=2
    )
    partials = [stacked[distance] for distance in range(reach)]
    carried = partials[STEPS]
    for distance in range(STEPS - 1, -1, -1):
        carried = from_behind(carried, "ctx", -1)
        carried = carried + partials[distance]
    conv_grad = jnp.concatenate([query_gradient_rows.reshape(tokens, 1, width), carried], axis=1)
    grad_edge = from_behind(conv_grad[: KW - 1], "ctx", -1)
    extended = jnp.concatenate([conv_grad, grad_edge], axis=0)
    input_grad = sum((filters[:, lag, :] * extended[lag : lag + tokens] for lag in range(KW)))
    tap_terms = jnp.stack(
        [
            jnp.sum(inputs[KW - 1 - lag : KW - 1 - lag + tokens] * conv_grad, axis=0)
            for lag in range(KW)
        ],
        axis=1,
    )
    filter_grad = lax.psum(tap_terms, "ctx")
    qkv_grad = lax.all_to_all(
        input_grad.astype(jnp.bfloat16), "tp", split_axis=0, concat_axis=2, tiled=True
    )
    return (attended.reshape(tokens, width), qkv_grad, filter_grad)


def solution(mesh):
    return jax.shard_map(
        shards,
        mesh=mesh,
        in_specs=(P(("ctx", "tp"), None, None), P(None, None, "tp"), P(), P("ctx", "tp")),
        out_specs=(P("ctx", "tp"), P(("ctx", "tp"), None, None), P(None, None, "tp")),
        check_vma=False,
    )
```

profile of v0, /device:TPU:0, one launch (start us, length us, event | category | flops | bytes accessed | tf_op | source)
XLA Modules:
  0.0 541.6 jit_solution(776772498163065581)
XLA Ops:
  7.2 10.7 %copy.57 = bf16[32,3,8192]{0,1,2:T(4,128)(2,1)} copy(bf16[32,3,8192]{2,0,1:T(8,128)(2,1)} %param.4) | data formatting | bytes 3145728 | tf_op args[0]
  17.8 8.4 %reshape.158 = bf16[4,2,98304]{2,1,0:T(2,128)(2,1)} reshape(bf16[8192,3,32]{2,1,0:T(4,128)(2,1)} %bitcast.114) | data formatting | bytes 3145728
  26.2 4.3 all-to-all-start
  30.7 19.9 %all-to-all-done = bf16[4,2,98304]{2,1,0:T(2,128)(2,1)S(1)} async-done(((bf16[4,2,98304]{2,1,0:T(2,128)(2,1)}), bf16[4,2,98304]{2,1,0:T(2,128)(2,1)S(1)}, u32[]{:S(2)}, u32[]{:S(2)}) %all-to-all-start) | async-done | bytes 1572896 | tf_op jit(solution)/shard_map/all_to_all | solution.py:25
  50.6 7.1 %reshape.159 = bf16[8192,3,32]{2,1,0:T(4,128)(2,1)} reshape(bf16[4,2,98304]{2,1,0:T(2,128)(2,1)S(1)} %all-to-all-done) | data formatting | bytes 3145728
  57.7 10.5 %copy.59 = bf16[4,32,3,2048]{3,1,0,2:T(8,128)(2,1)S(1)} copy(bf16[4,32,3,2048]{1,2,3,0:T(4,128)(2,1)} %bitcast.113) | data formatting | bytes 3145728 | tf_op jit(solution)/shard_map/all_to_all | solution.py:25
  68.2 4.2 collective-permute-start
  72.5 2.1 collective-permute-done
  74.7 1.9 maximum_convert_fusion
  76.6 2.6 add_convert_fusion
  79.2 1.1 copy-done.6
  80.4 1.1 fusion.49
  81.5 5.3 collective-permute-start.1
  86.8 20.0 %collective-permute-done.1 = bf16[128,2,2048]{2,0,1:T(8,128)(2,1)} collective-permute-done((bf16[128,2,2048]{2,0,1:T(8,128)(2,1)S(1)}, bf16[128,2,2048]{2,0,1:T(8,128)(2,1)}, u32[]{:S(2)}, u32[]{:S(2)}) %collective-permute-start.1) | collective-permute-done | bytes 1048608 | tf_op jit(solution)/shard_map/ppermute | solution.py:15
  106.8 5.5 %collective-permute-start.2 = (bf16[128,2,2048]{2,0,1:T(8,128)(2,1)}, bf16[128,2,2048]{2,0,1:T(8,128)(2,1)}, u32[]{:S(2)}, u32[]{:S(2)}) collective-permute-start(bf16[128,2,2048]{2,0,1:T(8,128)(2,1)} %collective-permute-done.1), channel_id=1, source_target_pairs={{0,4},{4,8},{8,12},{12,16},{16,20},{20,24},{24,28},{1,5},{5,9},{9,... | collective-permute-start | bytes 3145736 | tf_op jit(solution)/shard_map/ppermute | solution.py:15
  112.8 19.0 %collective-permute-done.2 = bf16[128,2,2048]{2,0,1:T(8,128)(2,1)} collective-permute-done((bf16[128,2,2048]{2,0,1:T(8,128)(2,1)}, bf16[128,2,2048]{2,0,1:T(8,128)(2,1)}, u32[]{:S(2)}, u32[]{:S(2)}) %collective-permute-start.2) | collective-permute-done | bytes 1048608 | tf_op jit(solution)/shard_map/ppermute | solution.py:15
  131.8 6.2 %collective-permute-start.3 = (bf16[128,2,2048]{2,0,1:T(8,128)(2,1)}, bf16[128,2,2048]{2,0,1:T(8,128)(2,1)}, u32[]{:S(2)}, u32[]{:S(2)}) collective-permute-start(bf16[128,2,2048]{2,0,1:T(8,128)(2,1)} %collective-permute-done.2), channel_id=1, source_target_pairs={{0,4},{4,8},{8,12},{12,16},{16,20},{20,24},{24,28},{1,5},{5,9},{9,... | collective-permute-start | bytes 3145736 | tf_op jit(solution)/shard_map/ppermute | solution.py:15
  141.8 14.7 %collective-permute-done.3 = bf16[128,2,2048]{2,0,1:T(8,128)(2,1)} collective-permute-done((bf16[128,2,2048]{2,0,1:T(8,128)(2,1)}, bf16[128,2,2048]{2,0,1:T(8,128)(2,1)}, u32[]{:S(2)}, u32[]{:S(2)}) %collective-permute-start.3) | collective-permute-done | bytes 1048608 | tf_op jit(solution)/shard_map/ppermute | solution.py:15
  156.5 6.3 %collective-permute-start.4 = (bf16[128,2,2048]{2,0,1:T(8,128)(2,1)}, bf16[128,2,2048]{2,0,1:T(8,128)(2,1)}, u32[]{:S(2)}, u32[]{:S(2)}) collective-permute-start(bf16[128,2,2048]{2,0,1:T(8,128)(2,1)} %collective-permute-done.3), channel_id=1, source_target_pairs={{0,4},{4,8},{8,12},{12,16},{16,20},{20,24},{24,28},{1,5},{5,9},{9,... | collective-permute-start | bytes 3145736 | tf_op jit(solution)/shard_map/ppermute | solution.py:15
  163.5 2.0 copy.65
  165.5 1.3 and_and_fusion
  166.9 1.9 slice.148
  168.8 2.0 copy.61
  170.8 2.3 constant_dynamic-update-slice_fusion.3
  173.1 2.3 constant_dynamic-update-slice_fusion.2
  175.4 2.3 constant_dynamic-update-slice_fusion.1
  177.8 2.6 collective-permute-done.4
  180.4 2.3 constant_dynamic-update-slice_fusion
  182.7 5.7 %fusion.48 = (bf16[640,1,2048]{2,0,1:T(8,128)(2,1)}, bf16[640,1,2048]{2,0,1:T(8,128)(2,1)}) fusion(bf16[640,2,2048]{2,0,1:T(8,128)(2,1)} %constant_dynamic-update-slice_fusion), kind=kLoop, calls=%fused_computation.106 | loop fusion | bytes 10485760 | tf_op jit(solution)/shard_map/slice | solution.py:47
  188.4 4.4 copy.62
  192.8 4.5 copy.60
  197.2 6.6 %fusion.52 = (f32[16,128]{1,0:T(8,128)S(1)}, f32[16,128,640]{2,1,0:T(8,128)}) fusion(pred[128,640]{1,0:T(8,128)(4,1)} %and_and_fusion, bf16[128,16,128]{0,2,1:T(8,128)(2,1)} %bitcast.124, bf16[640,16,128]{0,2,1:T(8,128)(2,1)} %bitcast.115), kind=kOutput, calls=%fused_computation.110 | convolution fusion | flops 342098560 | bytes 8478720 | tf_op jit(solution)/shard_map/sub | solution.py:71
  203.8 4.1 fusion.18
  208.9 1.8 multiply_reduce_fusion.7
  210.7 2.6 fusion.2
  213.3 5.3 copy.72
  218.6 6.8 %stack_reshape.7 = f32[5,128,1,2048]{3,1,0,2:T(8,128)} reshape(f32[640,16,128]{2,1,0:T(8,128)} %copy.72) | data formatting | bytes 10485760 | tf_op jit(solution)/shard_map/stack;reshape | solution.py:95
  225.4 5.0 convolution_bitcast_fusion
  230.5 7.4 %reshape.152 = f32[5,128,1,2048]{1,0,3,2:T(8,128)} reshape(f32[640,16,128]{0,2,1:T(8,128)} %convolution_bitcast_fusion) | data formatting | bytes 10485760 | tf_op jit(solution)/shard_map/stack;reshape | solution.py:95
  237.8 7.9 %copy.73 = f32[5,128,1,2048]{3,1,2,0:T(8,128)} copy(f32[5,128,1,2048]{1,0,3,2:T(8,128)} %reshape.152) | data formatting | bytes 10485760 | tf_op jit(solution)/shard_map/stack;reshape | solution.py:95
  245.7 1.8 fusion.25
  247.5 1.6 collective-permute-start.5
  249.1 44.7 %collective-permute-done.5 = f32[128,2,2048]{2,0,1:T(8,128)S(1)} collective-permute-done((f32[128,2,2048]{2,0,1:T(8,128)S(1)}, f32[128,2,2048]{2,0,1:T(8,128)S(1)}, u32[]{:S(2)}, u32[]{:S(2)}) %collective-permute-start.5) | collective-permute-done | bytes 2097184 | tf_op jit(solution)/shard_map/ppermute | solution.py:15
  294.2 1.5 collective-permute-start.6
  295.7 44.1 %collective-permute-done.6 = f32[128,2,2048]{2,0,1:T(8,128)S(1)} collective-permute-done((f32[128,2,2048]{2,0,1:T(8,128)S(1)}, f32[128,2,2048]{2,0,1:T(8,128)S(1)}, u32[]{:S(2)}, u32[]{:S(2)}) %collective-permute-start.6) | collective-permute-done | bytes 2097184 | tf_op jit(solution)/shard_map/ppermute | solution.py:15
  340.1 1.6 collective-permute-start.7
  341.7 42.9 %collective-permute-done.7 = f32[128,2,2048]{2,0,1:T(8,128)S(1)} collective-permute-done((f32[128,2,2048]{2,0,1:T(8,128)S(1)}, f32[128,2,2048]{2,0,1:T(8,128)S(1)}, u32[]{:S(2)}, u32[]{:S(2)}) %collective-permute-start.7) | collective-permute-done | bytes 2097184 | tf_op jit(solution)/shard_map/ppermute | solution.py:15
  384.5 1.6 fusion.23
  386.1 1.3 collective-permute-start.8
  387.4 2.1 fusion.53
  389.5 2.5 copy.75
  392.0 37.3 %collective-permute-done.8 = f32[128,2,2048]{2,0,1:T(8,128)} collective-permute-done((f32[128,2,2048]{2,0,1:T(8,128)}, f32[128,2,2048]{2,0,1:T(8,128)}, u32[]{:S(2)}, u32[]{:S(2)}) %collective-permute-start.8) | collective-permute-done | bytes 2097184 | tf_op jit(solution)/shard_map/ppermute | solution.py:15
  429.4 2.5 fusion.33
  431.9 3.6 multiply_reduce_fusion
  435.5 1.3 collective-permute-start.9
  437.5 6.2 %collective-permute-done.9 = f32[6,3,2048]{2,0,1:T(8,128)S(1)} collective-permute-done((f32[6,3,2048]{2,0,1:T(8,128)S(1)}, f32[6,3,2048]{2,0,1:T(8,128)S(1)}, u32[]{:S(2)}, u32[]{:S(2)}) %collective-permute-start.9) | collective-permute-done | bytes 147488 | tf_op jit(solution)/shard_map/ppermute | solution.py:15
  444.2 2.6 fusion.5
  446.9 2.7 copy.76
  449.5 3.7 all-to-all-start.1
  455.3 1.0 copy.79
  456.3 74.4 %all-reduce.2.cloned.1.call-done = f32[3,7,2048]{2,0,1:T(4,128)} async-done(((f32[3,7,2048]{2,0,1:T(4,128)}), f32[3,7,2048]{2,0,1:T(4,128)}) %all-reduce.2.cloned.1.call-update) | async-done | bytes 172048 | tf_op jit(solution)/shard_map/psum | solution.py:114
  530.7 1.7 copy.80
  532.4 1.1 copy.77
  533.5 1.2 copy.99
  (75 shorter events, 9.8 us)
Async XLA Ops:
  26.2 4.3 copy-start.13
  26.2 24.4 %all-to-all-start = ((bf16[4,2,98304]{2,1,0:T(2,128)(2,1)}), bf16[4,2,98304]{2,1,0:T(2,128)(2,1)S(1)}, u32[]{:S(2)}, u32[]{:S(2)}) async-start(bf16[4,2,98304]{2,1,0:T(2,128)(2,1)} %reshape.158), calls=%async_computation | async-start | bytes 3145728 | tf_op jit(solution)/shard_map/all_to_all | solution.py:25
  68.2 4.3 copy-start.5
  68.2 6.4 %collective-permute-start = (bf16[6,3,2048]{2,0,1:T(8,128)(2,1)S(1)}, bf16[6,3,2048]{2,0,1:T(8,128)(2,1)S(1)}, u32[]{:S(2)}, u32[]{:S(2)}) collective-permute-start(bf16[6,3,2048]{2,0,1:T(8,128)(2,1)S(1)} %slice.138), channel_id=1, source_target_pairs={{0,4},{4,8},{8,12},{12,16},{16,20},{20,24},{24,28},{1,5},{5,9},{9,... | collective-permute-start | bytes 221192 | tf_op jit(solution)/shard_map/ppermute | solution.py:15
  72.5 6.7 %copy-start.11 = (f32[3,1,2048]{2,0,1:T(4,128)}, f32[3,1,2048]{2,0,1:T(4,128)S(1)}, u32[]{:S(2)}) copy-start(f32[3,1,2048]{2,0,1:T(4,128)S(1)} %copy.107) | copy-start | bytes 73732
  79.2 1.1 copy-start.6
  80.4 57.7 %copy-start.17 = (s32[8]{0:T(128)S(1)}, s32[8]{0:T(128)}, u32[]{:S(2)}) copy-start(s32[8]{0:T(128)} %param.6) | copy-start | bytes 100
  81.5 25.4 %collective-permute-start.1 = (bf16[128,2,2048]{2,0,1:T(8,128)(2,1)S(1)}, bf16[128,2,2048]{2,0,1:T(8,128)(2,1)}, u32[]{:S(2)}, u32[]{:S(2)}) collective-permute-start(bf16[128,2,2048]{2,0,1:T(8,128)(2,1)S(1)} %get-tuple-element.24), channel_id=1, source_target_pairs={{0,4},{4,8},{8,12},{12,16},{16,20},{20,24},{24,28},{1,5},{5,9},{9,... | collective-permute-start | bytes 3145736 | tf_op jit(solution)/shard_map/ppermute | solution.py:15
  106.8 24.9 %collective-permute-start.2 = (bf16[128,2,2048]{2,0,1:T(8,128)(2,1)}, bf16[128,2,2048]{2,0,1:T(8,128)(2,1)}, u32[]{:S(2)}, u32[]{:S(2)}) collective-permute-start(bf16[128,2,2048]{2,0,1:T(8,128)(2,1)} %collective-permute-done.1), channel_id=1, source_target_pairs={{0,4},{4,8},{8,12},{12,16},{16,20},{20,24},{24,28},{1,5},{5,9},{9,... | collective-permute-start | bytes 3145736 | tf_op jit(solution)/shard_map/ppermute | solution.py:15
  131.8 24.7 %collective-permute-start.3 = (bf16[128,2,2048]{2,0,1:T(8,128)(2,1)}, bf16[128,2,2048]{2,0,1:T(8,128)(2,1)}, u32[]{:S(2)}, u32[]{:S(2)}) collective-permute-start(bf16[128,2,2048]{2,0,1:T(8,128)(2,1)} %collective-permute-done.2), channel_id=1, source_target_pairs={{0,4},{4,8},{8,12},{12,16},{16,20},{20,24},{24,28},{1,5},{5,9},{9,... | collective-permute-start | bytes 3145736 | tf_op jit(solution)/shard_map/ppermute | solution.py:15
  156.5 23.9 %collective-permute-start.4 = (bf16[128,2,2048]{2,0,1:T(8,128)(2,1)}, bf16[128,2,2048]{2,0,1:T(8,128)(2,1)}, u32[]{:S(2)}, u32[]{:S(2)}) collective-permute-start(bf16[128,2,2048]{2,0,1:T(8,128)(2,1)} %collective-permute-done.3), channel_id=1, source_target_pairs={{0,4},{4,8},{8,12},{12,16},{16,20},{20,24},{24,28},{1,5},{5,9},{9,... | collective-permute-start | bytes 3145736 | tf_op jit(solution)/shard_map/ppermute | solution.py:15
  203.8 4.1 copy-start.4
  203.8 5.0 copy-start.7
  203.8 5.0 copy-start.9
  245.7 48.1 %slice-start = ((s8[5242880]{0:T(1024)(128)(4,1)}), s8[4194304]{0:T(1024)(128)(4,1)S(1)}, s32[]{:S(2)}) async-start(s8[5242880]{0:T(1024)(128)(4,1)} %bitcast.108), calls=%async_computation.3 | async-start | bytes 8388608
  245.7 48.1 %slice-start.1 = ((s8[5242880]{0:T(1024)(128)(4,1)}), s8[1048576]{0:T(1024)(128)(4,1)S(1)}, s32[]{:S(2)}) async-start(s8[5242880]{0:T(1024)(128)(4,1)} %bitcast.108), calls=%async_computation.4 | async-start | bytes 2097152
  245.7 48.1 %copy-start = (f32[5,128,1,2048]{3,1,2,0:T(8,128)S(1)}, f32[5,128,1,2048]{3,1,2,0:T(8,128)}, u32[]{:S(2)}) copy-start(f32[5,128,1,2048]{3,1,2,0:T(8,128)} %copy.73) | copy-start | bytes 15728644
  247.5 46.3 %collective-permute-start.5 = (f32[128,2,2048]{2,0,1:T(8,128)S(1)}, f32[128,2,2048]{2,0,1:T(8,128)S(1)}, u32[]{:S(2)}, u32[]{:S(2)}) collective-permute-start(f32[128,2,2048]{2,0,1:T(8,128)S(1)} %fusion.25), channel_id=1, source_target_pairs={{4,0},{8,4},{12,8},{16,12},{20,16},{24,20},{28,24},{5,1},{9,5},{13... | collective-permute-start | bytes 6291464 | tf_op jit(solution)/shard_map/ppermute | solution.py:15
  294.2 45.6 %collective-permute-start.6 = (f32[128,2,2048]{2,0,1:T(8,128)S(1)}, f32[128,2,2048]{2,0,1:T(8,128)S(1)}, u32[]{:S(2)}, u32[]{:S(2)}) collective-permute-start(f32[128,2,2048]{2,0,1:T(8,128)S(1)} %fusion.28), channel_id=1, source_target_pairs={{4,0},{8,4},{12,8},{16,12},{20,16},{24,20},{28,24},{5,1},{9,5},{13... | collective-permute-start | bytes 6291464 | tf_op jit(solution)/shard_map/ppermute | solution.py:15
  340.1 47.3 %copy-start.2 = (bf16[640,1,2048]{0,2,1:T(8,128)(2,1)S(1)}, bf16[640,1,2048]{0,2,1:T(8,128)(2,1)}, u32[]{:S(2)}) copy-start(bf16[640,1,2048]{0,2,1:T(8,128)(2,1)} %copy.62) | copy-start | bytes 7864324
  340.1 47.3 %copy-start.3 = (bf16[16,128,640]{2,1,0:T(8,128)(2,1)S(1)}, bf16[16,128,640]{2,1,0:T(8,128)(2,1)}, u32[]{:S(2)}) copy-start(bf16[16,128,640]{2,1,0:T(8,128)(2,1)} %fusion.2) | copy-start | bytes 7864324
  340.1 44.4 %collective-permute-start.7 = (f32[128,2,2048]{2,0,1:T(8,128)S(1)}, f32[128,2,2048]{2,0,1:T(8,128)S(1)}, u32[]{:S(2)}, u32[]{:S(2)}) collective-permute-start(f32[128,2,2048]{2,0,1:T(8,128)S(1)} %fusion.31), channel_id=1, source_target_pairs={{4,0},{8,4},{12,8},{16,12},{20,16},{24,20},{28,24},{5,1},{9,5},{13... | collective-permute-start | bytes 6291464 | tf_op jit(solution)/shard_map/ppermute | solution.py:15
  386.1 43.2 %collective-permute-start.8 = (f32[128,2,2048]{2,0,1:T(8,128)}, f32[128,2,2048]{2,0,1:T(8,128)}, u32[]{:S(2)}, u32[]{:S(2)}) collective-permute-start(f32[128,2,2048]{2,0,1:T(8,128)} %fusion.23), channel_id=1, source_target_pairs={{4,0},{8,4},{12,8},{16,12},{20,16},{24,20},{28,24},{5,1},{9,5},{13... | collective-permute-start | bytes 6291464 | tf_op jit(solution)/shard_map/ppermute | solution.py:15
  392.0 39.8 %copy-start.1 = (f32[128,1,2048]{2,0,1:T(8,128)S(1)}, f32[128,1,2048]{2,0,1:T(8,128)}, u32[]{:S(2)}) copy-start(f32[128,1,2048]{2,0,1:T(8,128)} %copy.75) | copy-start | bytes 3145732
  435.5 8.3 %collective-permute-start.9 = (f32[6,3,2048]{2,0,1:T(8,128)S(1)}, f32[6,3,2048]{2,0,1:T(8,128)S(1)}, u32[]{:S(2)}, u32[]{:S(2)}) collective-permute-start(f32[6,3,2048]{2,0,1:T(8,128)S(1)} %fusion.45), channel_id=1, source_target_pairs={{4,0},{8,4},{12,8},{16,12},{20,16},{24,20},{28,24},{5,1},{9,5},{13... | collective-permute-start | bytes 442376 | tf_op jit(solution)/shard_map/ppermute | solution.py:15
  436.8 0.7 copy-start.10
  437.5 6.6 %copy-start.12 = (f32[3,1,2048]{2,0,1:T(4,128)S(1)}, f32[3,1,2048]{2,0,1:T(4,128)}, u32[]{:S(2)}) copy-start(f32[3,1,2048]{2,0,1:T(4,128)} %copy-done.11) | copy-start | bytes 73732
  446.8 6.5 %copy-start.16 = (f32[3,2048]{1,0:T(4,128)S(1)}, f32[3,2048]{1,0:T(4,128)}, u32[]{:S(2)}) copy-start(f32[3,2048]{1,0:T(4,128)} %get-tuple-element.17) | copy-start | bytes 73732
  446.8 7.2 %copy-start.15 = (f32[3,2048]{1,0:T(4,128)S(1)}, f32[3,2048]{1,0:T(4,128)}, u32[]{:S(2)}) copy-start(f32[3,2048]{1,0:T(4,128)} %get-tuple-element.16) | copy-start | bytes 73732
  446.8 7.8 %copy-start.14 = (f32[3,2048]{1,0:T(4,128)S(1)}, f32[3,2048]{1,0:T(4,128)}, u32[]{:S(2)}) copy-start(f32[3,2048]{1,0:T(4,128)} %get-tuple-element.15) | copy-start | bytes 73732
  449.5 5.7 %copy-start.8 = (bf16[128,16,128]{0,2,1:T(8,128)(2,1)S(1)}, bf16[128,16,128]{0,2,1:T(8,128)(2,1)}, u32[]{:S(2)}) copy-start(bf16[128,16,128]{0,2,1:T(8,128)(2,1)} %get-tuple-element.41) | copy-start | bytes 1572868
  449.5 82.8 %all-to-all-start.1 = ((bf16[128,3,2048]{2,1,0:T(4,128)(2,1)}), bf16[128,3,2048]{2,1,0:T(4,128)(2,1)S(1)}, u32[]{:S(2)}, u32[]{:S(2)}) async-start(bf16[128,3,2048]{2,1,0:T(4,128)(2,1)} %copy.76), calls=%async_computation.1 | async-start | bytes 4194304 | tf_op jit(solution)/shard_map/all_to_all | solution.py:115
  453.3 77.4 %all-reduce.2.cloned.1.call-start = ((), (), s32[]{:S(2)}) async-start(), calls=%async_computation.2 | async-start | bytes 458752 | tf_op jit(solution)/shard_map/psum | solution.py:114
Sparse Core Ops, SparseCore 0:
  458.1 72.5 all-reduce.1
where the time goes:
time: 544 us; the launch traced here: 542 us
  waiting for transfers between devices  328 us (60%)
  local copies, waits for them, and re-layouts  114 us (21%)
  starting transfers between devices  42.9 us (8%)
  matrix products  22.2 us (4%)
  other arithmetic  20.2 us (4%)
  between operations  14.5 us (3%)
    ppermute x10, waiting for transfers between devices, from_behind(): lax.ppermute(value, axis, [(source, source + steps) for source in range(f...  234 us
    psum x1, waiting for transfers between devices, shards(): filter_grad = lax.psum(tap_terms, 'ctx')  74.4 us
    unnamed x63, local copies, waits for them, and re-layouts  44.5 us
    ppermute x10, starting transfers between devices, from_behind(): lax.ppermute(value, axis, [(source, source + steps) for source in range(f...  34.8 us
    another operation x3, local copies, waits for them, and re-layouts, shards(): jnp.stack([key_part.reshape(reach, tokens, width), value_part.reshape(rea...  22 us
    all_to_all x1, waiting for transfers between devices, shards(): local = lax.all_to_all(qkv, 'tp', split_axis=2, concat_axis=0, tiled=True)  19.9 us
  transfers between devices with their start and end apart: 13, of which 12 were waited for; matrix products, arithmetic and copies ran while one was open for 5% of the time, Pallas kernels for 0%

commit v1 on v0

--- a/solution.py
+++ b/solution.py
@@ -111,7 +111,11 @@
         ],
         axis=1,
     )
-    filter_grad = lax.psum(tap_terms, "ctx")
+    filter_grad = tap_terms
+    for hop in (1, 2, 4):
+        filter_grad = filter_grad + lax.ppermute(
+            filter_grad, "ctx", [(dev, dev ^ hop) for dev in range(8)]
+        )
     qkv_grad = lax.all_to_all(
         input_grad.astype(jnp.bfloat16), "tp", split_axis=0, concat_axis=2, tiled=True
     )

time: 544 us -> 481 us (0.88)
  waiting for transfers between devices: 328 us -> 274 us
  between operations: 14.5 us -> 1.11 us
  starting transfers between devices: 42.9 us -> 50.1 us
    psum x1 -> x0, waiting for transfers between devices: 74.4 us -> none  [shards(): filter_grad = lax.psum(tap_terms, 'ctx')]
    ppermute x0 -> x3, waiting for transfers between devices: none -> 20.7 us  [shards(): lax.ppermute(filter_grad, 'ctx', [(dev, dev ^ hop) for dev in range(8)])]
    ppermute x0 -> x3, starting transfers between devices: none -> 7.28 us  [shards(): lax.ppermute(filter_grad, 'ctx', [(dev, dev ^ hop) for dev in range(8)])]
  transfers between devices with their start and end apart: 13 -> 15, of which waited for: 12 -> 14; matrix products, arithmetic and copies ran while one was open for 5% -> 5% of each run, Pallas kernels for 0% -> 0%
where the time goes in v1:
time: 481 us; the launch traced here: 479 us
  waiting for transfers between devices  274 us (57%)
  local copies, waits for them, and re-layouts  111 us (23%)
  starting transfers between devices  50.1 us (10%)
  matrix products  22.2 us (5%)
  other arithmetic  20.4 us (4%)
    ppermute x10, waiting for transfers between devices, from_behind(): lax.ppermute(value, axis, [(source, source + steps) for source in range(f...  233 us
    unnamed x63, local copies, waits for them, and re-layouts  42.4 us
    ppermute x10, starting transfers between devices, from_behind(): lax.ppermute(value, axis, [(source, source + steps) for source in range(f...  34.8 us
    another operation x3, local copies, waits for them, and re-layouts, shards(): jnp.stack([key_part.reshape(reach, tokens, width), value_part.reshape(rea...  21.9 us
    ppermute x3, waiting for transfers between devices, shards(): lax.ppermute(filter_grad, 'ctx', [(dev, dev ^ hop) for dev in range(8)])  20.7 us
    all_to_all x1, waiting for transfers between devices, shards(): local = lax.all_to_all(qkv, 'tp', split_axis=2, concat_axis=0, tiled=True)  19.9 us
    all_to_all x1, local copies, waits for them, and re-layouts, shards(): local = lax.all_to_all(qkv, 'tp', split_axis=2, concat_axis=0, tiled=True)  10.5 us
    slice x2, local copies, waits for them, and re-layouts, shards(): keys = joined[:, 0].reshape(reach * tokens, heads, HEAD_DIM)  10.1 us
  transfers between devices with their start and end apart: 15, of which 14 were waited for; matrix products, arithmetic and copies ran while one was open for 5% of the time, Pallas kernels for 0%

profile of v1, /device:TPU:0, one launch (start us, length us, event | category | flops | bytes accessed | tf_op | source)
XLA Modules:
  0.0 479.3 jit_solution(15907256021810353618)
XLA Ops:
  0.6 10.6 %copy.57 = bf16[32,3,8192]{0,1,2:T(4,128)(2,1)} copy(bf16[32,3,8192]{2,0,1:T(8,128)(2,1)} %param.4) | data formatting | bytes 3145728 | tf_op args[0]
  11.3 8.4 %reshape.158 = bf16[4,2,98304]{2,1,0:T(2,128)(2,1)} reshape(bf16[8192,3,32]{2,1,0:T(4,128)(2,1)} %bitcast.114) | data formatting | bytes 3145728
  19.6 4.3 all-to-all-start
  24.2 19.9 %all-to-all-done = bf16[4,2,98304]{2,1,0:T(2,128)(2,1)S(1)} async-done(((bf16[4,2,98304]{2,1,0:T(2,128)(2,1)}), bf16[4,2,98304]{2,1,0:T(2,128)(2,1)S(1)}, u32[]{:S(2)}, u32[]{:S(2)}) %all-to-all-start) | async-done | bytes 1572896 | tf_op jit(solution)/shard_map/all_to_all | solution.py:25
  44.1 7.1 %reshape.159 = bf16[8192,3,32]{2,1,0:T(4,128)(2,1)} reshape(bf16[4,2,98304]{2,1,0:T(2,128)(2,1)S(1)} %all-to-all-done) | data formatting | bytes 3145728
  51.1 10.5 %copy.59 = bf16[4,32,3,2048]{3,1,0,2:T(8,128)(2,1)S(1)} copy(bf16[4,32,3,2048]{1,2,3,0:T(4,128)(2,1)} %bitcast.113) | data formatting | bytes 3145728 | tf_op jit(solution)/shard_map/all_to_all | solution.py:25
  61.7 4.2 collective-permute-start
  66.0 2.1 collective-permute-done
  68.1 1.9 maximum_convert_fusion
  70.0 2.6 add_convert_fusion
  75.0 5.3 %collective-permute-start.1 = (bf16[128,2,2048]{2,0,1:T(8,128)(2,1)S(1)}, bf16[128,2,2048]{2,0,1:T(8,128)(2,1)}, u32[]{:S(2)}, u32[]{:S(2)}) collective-permute-start(bf16[128,2,2048]{2,0,1:T(8,128)(2,1)S(1)} %get-tuple-element.24), channel_id=1, source_target_pairs={{0,4},{4,8},{8,12},{12,16},{16,20},{20,24},{24,28},{1,5},{5,9},{9,... | collective-permute-start | bytes 3145736 | tf_op jit(solution)/shard_map/ppermute | solution.py:15
  80.3 20.0 %collective-permute-done.1 = bf16[128,2,2048]{2,0,1:T(8,128)(2,1)} collective-permute-done((bf16[128,2,2048]{2,0,1:T(8,128)(2,1)S(1)}, bf16[128,2,2048]{2,0,1:T(8,128)(2,1)}, u32[]{:S(2)}, u32[]{:S(2)}) %collective-permute-start.1) | collective-permute-done | bytes 1048608 | tf_op jit(solution)/shard_map/ppermute | solution.py:15
  100.3 5.5 %collective-permute-start.2 = (bf16[128,2,2048]{2,0,1:T(8,128)(2,1)}, bf16[128,2,2048]{2,0,1:T(8,128)(2,1)}, u32[]{:S(2)}, u32[]{:S(2)}) collective-permute-start(bf16[128,2,2048]{2,0,1:T(8,128)(2,1)} %collective-permute-done.1), channel_id=1, source_target_pairs={{0,4},{4,8},{8,12},{12,16},{16,20},{20,24},{24,28},{1,5},{5,9},{9,... | collective-permute-start | bytes 3145736 | tf_op jit(solution)/shard_map/ppermute | solution.py:15
  106.3 18.9 %collective-permute-done.2 = bf16[128,2,2048]{2,0,1:T(8,128)(2,1)} collective-permute-done((bf16[128,2,2048]{2,0,1:T(8,128)(2,1)}, bf16[128,2,2048]{2,0,1:T(8,128)(2,1)}, u32[]{:S(2)}, u32[]{:S(2)}) %collective-permute-start.2) | collective-permute-done | bytes 1048608 | tf_op jit(solution)/shard_map/ppermute | solution.py:15
  125.3 6.2 %collective-permute-start.3 = (bf16[128,2,2048]{2,0,1:T(8,128)(2,1)}, bf16[128,2,2048]{2,0,1:T(8,128)(2,1)}, u32[]{:S(2)}, u32[]{:S(2)}) collective-permute-start(bf16[128,2,2048]{2,0,1:T(8,128)(2,1)} %collective-permute-done.2), channel_id=1, source_target_pairs={{0,4},{4,8},{8,12},{12,16},{16,20},{20,24},{24,28},{1,5},{5,9},{9,... | collective-permute-start | bytes 3145736 | tf_op jit(solution)/shard_map/ppermute | solution.py:15
  135.5 14.5 %collective-permute-done.3 = bf16[128,2,2048]{2,0,1:T(8,128)(2,1)} collective-permute-done((bf16[128,2,2048]{2,0,1:T(8,128)(2,1)}, bf16[128,2,2048]{2,0,1:T(8,128)(2,1)}, u32[]{:S(2)}, u32[]{:S(2)}) %collective-permute-start.3) | collective-permute-done | bytes 1048608 | tf_op jit(solution)/shard_map/ppermute | solution.py:15
  150.0 6.4 %collective-permute-start.4 = (bf16[128,2,2048]{2,0,1:T(8,128)(2,1)}, bf16[128,2,2048]{2,0,1:T(8,128)(2,1)}, u32[]{:S(2)}, u32[]{:S(2)}) collective-permute-start(bf16[128,2,2048]{2,0,1:T(8,128)(2,1)} %collective-permute-done.3), channel_id=1, source_target_pairs={{0,4},{4,8},{8,12},{12,16},{16,20},{20,24},{24,28},{1,5},{5,9},{9,... | collective-permute-start | bytes 3145736 | tf_op jit(solution)/shard_map/ppermute | solution.py:15
  157.0 2.0 copy.65
  159.0 1.4 and_and_fusion
  160.4 1.9 slice.148
  162.3 2.0 copy.61
  164.3 2.3 constant_dynamic-update-slice_fusion.3
  166.6 2.3 constant_dynamic-update-slice_fusion.2
  169.0 2.3 constant_dynamic-update-slice_fusion.1
  171.3 2.6 collective-permute-done.4
  173.9 2.3 constant_dynamic-update-slice_fusion
  176.2 5.7 %fusion.48 = (bf16[640,1,2048]{2,0,1:T(8,128)(2,1)}, bf16[640,1,2048]{2,0,1:T(8,128)(2,1)}) fusion(bf16[640,2,2048]{2,0,1:T(8,128)(2,1)} %constant_dynamic-update-slice_fusion), kind=kLoop, calls=%fused_computation.106 | loop fusion | bytes 10485760 | tf_op jit(solution)/shard_map/slice | solution.py:47
  181.9 4.4 copy.62
  186.3 4.5 copy.60
  190.8 6.6 %fusion.52 = (f32[16,128]{1,0:T(8,128)S(1)}, f32[16,128,640]{2,1,0:T(8,128)}) fusion(pred[128,640]{1,0:T(8,128)(4,1)} %and_and_fusion, bf16[128,16,128]{0,2,1:T(8,128)(2,1)} %bitcast.124, bf16[640,16,128]{0,2,1:T(8,128)(2,1)} %bitcast.115), kind=kOutput, calls=%fused_computation.110 | convolution fusion | flops 342098560 | bytes 8478720 | tf_op jit(solution)/shard_map/sub | solution.py:71
  197.4 4.1 fusion.18
  202.4 1.8 multiply_reduce_fusion.7
  204.3 2.6 fusion.2
  206.9 5.4 %copy.72 = f32[640,16,128]{2,1,0:T(8,128)} copy(f32[640,16,128]{2,0,1:T(8,128)S(1)} %fusion.18) | data formatting | bytes 10485760 | tf_op jit(solution)/shard_map/hqk,qhd->khd/transpose | solution.py:80
  212.2 6.8 %stack_reshape.7 = f32[5,128,1,2048]{3,1,0,2:T(8,128)} reshape(f32[640,16,128]{2,1,0:T(8,128)} %copy.72) | data formatting | bytes 10485760 | tf_op jit(solution)/shard_map/stack;reshape | solution.py:95
  219.0 5.0 %convolution_bitcast_fusion = f32[640,16,128]{0,2,1:T(8,128)} fusion(bf16[128,16,128]{0,2,1:T(8,128)(2,1)} %bitcast.125, bf16[16,128,640]{2,1,0:T(8,128)(2,1)} %fusion.2), kind=kOutput, calls=%fused_computation.48 | convolution fusion | flops 335544320 | bytes 8388608 | tf_op jit(solution)/shard_map/hqk,qhd->khd/dot_general | solution.py:92
  224.0 7.3 %reshape.152 = f32[5,128,1,2048]{1,0,3,2:T(8,128)} reshape(f32[640,16,128]{0,2,1:T(8,128)} %convolution_bitcast_fusion) | data formatting | bytes 10485760 | tf_op jit(solution)/shard_map/stack;reshape | solution.py:95
  231.4 7.8 %copy.73 = f32[5,128,1,2048]{3,1,2,0:T(8,128)} copy(f32[5,128,1,2048]{1,0,3,2:T(8,128)} %reshape.152) | data formatting | bytes 10485760 | tf_op jit(solution)/shard_map/stack;reshape | solution.py:95
  239.2 1.8 fusion.25
  241.0 1.6 collective-permute-start.5
  242.6 44.7 %collective-permute-done.5 = f32[128,2,2048]{2,0,1:T(8,128)S(1)} collective-permute-done((f32[128,2,2048]{2,0,1:T(8,128)S(1)}, f32[128,2,2048]{2,0,1:T(8,128)S(1)}, u32[]{:S(2)}, u32[]{:S(2)}) %collective-permute-start.5) | collective-permute-done | bytes 2097184 | tf_op jit(solution)/shard_map/ppermute | solution.py:15
  287.7 1.5 collective-permute-start.6
  289.2 44.1 %collective-permute-done.6 = f32[128,2,2048]{2,0,1:T(8,128)S(1)} collective-permute-done((f32[128,2,2048]{2,0,1:T(8,128)S(1)}, f32[128,2,2048]{2,0,1:T(8,128)S(1)}, u32[]{:S(2)}, u32[]{:S(2)}) %collective-permute-start.6) | collective-permute-done | bytes 2097184 | tf_op jit(solution)/shard_map/ppermute | solution.py:15
  333.6 1.6 collective-permute-start.7
  335.2 42.9 %collective-permute-done.7 = f32[128,2,2048]{2,0,1:T(8,128)S(1)} collective-permute-done((f32[128,2,2048]{2,0,1:T(8,128)S(1)}, f32[128,2,2048]{2,0,1:T(8,128)S(1)}, u32[]{:S(2)}, u32[]{:S(2)}) %collective-permute-start.7) | collective-permute-done | bytes 2097184 | tf_op jit(solution)/shard_map/ppermute | solution.py:15
  378.1 1.6 fusion.23
  379.6 1.3 collective-permute-start.8
  380.9 2.1 fusion.53
  383.0 2.5 copy.75
  385.5 37.3 %collective-permute-done.8 = f32[128,2,2048]{2,0,1:T(8,128)} collective-permute-done((f32[128,2,2048]{2,0,1:T(8,128)}, f32[128,2,2048]{2,0,1:T(8,128)}, u32[]{:S(2)}, u32[]{:S(2)}) %collective-permute-start.8) | collective-permute-done | bytes 2097184 | tf_op jit(solution)/shard_map/ppermute | solution.py:15
  422.9 2.5 fusion.33
  425.4 3.6 multiply_reduce_fusion
  429.0 1.3 collective-permute-start.9
  431.1 6.2 %collective-permute-done.9 = f32[6,3,2048]{2,0,1:T(8,128)S(1)} collective-permute-done((f32[6,3,2048]{2,0,1:T(8,128)S(1)}, f32[6,3,2048]{2,0,1:T(8,128)S(1)}, u32[]{:S(2)}, u32[]{:S(2)}) %collective-permute-start.9) | collective-permute-done | bytes 147488 | tf_op jit(solution)/shard_map/ppermute | solution.py:15
  437.7 2.6 fusion.5
  440.4 2.7 copy.76
  443.1 3.7 all-to-all-start.1
  446.9 3.0 collective-permute-start.10
  449.9 6.2 %collective-permute-done.10 = f32[3,7,2048]{2,0,1:T(4,128)S(1)} collective-permute-done((f32[3,7,2048]{2,0,1:T(4,128)S(1)}, f32[3,7,2048]{2,0,1:T(4,128)S(1)}, u32[]{:S(2)}, u32[]{:S(2)}) %collective-permute-start.10) | collective-permute-done | bytes 172064 | tf_op jit(solution)/shard_map/ppermute | solution.py:116
  456.1 1.6 collective-permute-start.11
  457.8 5.8 %collective-permute-done.11 = f32[3,7,2048]{2,0,1:T(4,128)S(1)} collective-permute-done((f32[3,7,2048]{2,0,1:T(4,128)S(1)}, f32[3,7,2048]{2,0,1:T(4,128)S(1)}, u32[]{:S(2)}, u32[]{:S(2)}) %collective-permute-start.11) | collective-permute-done | bytes 172064 | tf_op jit(solution)/shard_map/ppermute | solution.py:116
  463.7 2.7 collective-permute-start.12
  467.3 8.7 %collective-permute-done.12 = f32[3,7,2048]{2,0,1:T(4,128)S(1)} collective-permute-done((f32[3,7,2048]{2,0,1:T(4,128)S(1)}, f32[3,7,2048]{2,0,1:T(4,128)S(1)}, u32[]{:S(2)}, u32[]{:S(2)}) %collective-permute-start.12) | collective-permute-done | bytes 172064 | tf_op jit(solution)/shard_map/ppermute | solution.py:116
  478.0 1.2 copy.99
  (81 shorter events, 13.5 us)
Async XLA Ops:
  19.6 4.3 copy-start.14
  19.6 24.4 %all-to-all-start = ((bf16[4,2,98304]{2,1,0:T(2,128)(2,1)}), bf16[4,2,98304]{2,1,0:T(2,128)(2,1)S(1)}, u32[]{:S(2)}, u32[]{:S(2)}) async-start(bf16[4,2,98304]{2,1,0:T(2,128)(2,1)} %reshape.158), calls=%async_computation | async-start | bytes 3145728 | tf_op jit(solution)/shard_map/all_to_all | solution.py:25
  61.7 4.3 copy-start.5
  61.7 6.4 %collective-permute-start = (bf16[6,3,2048]{2,0,1:T(8,128)(2,1)S(1)}, bf16[6,3,2048]{2,0,1:T(8,128)(2,1)S(1)}, u32[]{:S(2)}, u32[]{:S(2)}) collective-permute-start(bf16[6,3,2048]{2,0,1:T(8,128)(2,1)S(1)} %slice.138), channel_id=1, source_target_pairs={{0,4},{4,8},{8,12},{12,16},{16,20},{20,24},{24,28},{1,5},{5,9},{9,... | collective-permute-start | bytes 221192 | tf_op jit(solution)/shard_map/ppermute | solution.py:15
  66.0 6.7 %copy-start.12 = (f32[3,1,2048]{2,0,1:T(4,128)}, f32[3,1,2048]{2,0,1:T(4,128)S(1)}, u32[]{:S(2)}) copy-start(f32[3,1,2048]{2,0,1:T(4,128)S(1)} %copy.107) | copy-start | bytes 73732
  72.7 1.1 copy-start.6
  73.8 57.7 %copy-start.17 = (s32[8]{0:T(128)S(1)}, s32[8]{0:T(128)}, u32[]{:S(2)}) copy-start(s32[8]{0:T(128)} %param.6) | copy-start | bytes 100
  75.0 25.4 %collective-permute-start.1 = (bf16[128,2,2048]{2,0,1:T(8,128)(2,1)S(1)}, bf16[128,2,2048]{2,0,1:T(8,128)(2,1)}, u32[]{:S(2)}, u32[]{:S(2)}) collective-permute-start(bf16[128,2,2048]{2,0,1:T(8,128)(2,1)S(1)} %get-tuple-element.24), channel_id=1, source_target_pairs={{0,4},{4,8},{8,12},{12,16},{16,20},{20,24},{24,28},{1,5},{5,9},{9,... | collective-permute-start | bytes 3145736 | tf_op jit(solution)/shard_map/ppermute | solution.py:15
  100.3 24.9 %collective-permute-start.2 = (bf16[128,2,2048]{2,0,1:T(8,128)(2,1)}, bf16[128,2,2048]{2,0,1:T(8,128)(2,1)}, u32[]{:S(2)}, u32[]{:S(2)}) collective-permute-start(bf16[128,2,2048]{2,0,1:T(8,128)(2,1)} %collective-permute-done.1), channel_id=1, source_target_pairs={{0,4},{4,8},{8,12},{12,16},{16,20},{20,24},{24,28},{1,5},{5,9},{9,... | collective-permute-start | bytes 3145736 | tf_op jit(solution)/shard_map/ppermute | solution.py:15
  125.3 24.7 %collective-permute-start.3 = (bf16[128,2,2048]{2,0,1:T(8,128)(2,1)}, bf16[128,2,2048]{2,0,1:T(8,128)(2,1)}, u32[]{:S(2)}, u32[]{:S(2)}) collective-permute-start(bf16[128,2,2048]{2,0,1:T(8,128)(2,1)} %collective-permute-done.2), channel_id=1, source_target_pairs={{0,4},{4,8},{8,12},{12,16},{16,20},{20,24},{24,28},{1,5},{5,9},{9,... | collective-permute-start | bytes 3145736 | tf_op jit(solution)/shard_map/ppermute | solution.py:15
  150.0 23.9 %collective-permute-start.4 = (bf16[128,2,2048]{2,0,1:T(8,128)(2,1)}, bf16[128,2,2048]{2,0,1:T(8,128)(2,1)}, u32[]{:S(2)}, u32[]{:S(2)}) collective-permute-start(bf16[128,2,2048]{2,0,1:T(8,128)(2,1)} %collective-permute-done.3), channel_id=1, source_target_pairs={{0,4},{4,8},{8,12},{12,16},{16,20},{20,24},{24,28},{1,5},{5,9},{9,... | collective-permute-start | bytes 3145736 | tf_op jit(solution)/shard_map/ppermute | solution.py:15
  197.4 4.1 copy-start.4
  197.4 5.0 %copy-start.7 = (f32[16,128,640]{2,1,0:T(8,128)S(1)}, f32[16,128,640]{2,1,0:T(8,128)}, u32[]{:S(2)}) copy-start(f32[16,128,640]{2,1,0:T(8,128)} %get-tuple-element.39) | copy-start | bytes 15728644
  197.4 5.0 %copy-start.9 = (bf16[128,2048]{0,1:T(8,128)(2,1)S(1)}, bf16[128,2048]{0,1:T(8,128)(2,1)}, u32[]{:S(2)}) copy-start(bf16[128,2048]{0,1:T(8,128)(2,1)} %copy.65) | copy-start | bytes 1572868
  239.2 48.1 %slice-start = ((s8[5242880]{0:T(1024)(128)(4,1)}), s8[4194304]{0:T(1024)(128)(4,1)S(1)}, s32[]{:S(2)}) async-start(s8[5242880]{0:T(1024)(128)(4,1)} %bitcast.108), calls=%async_computation.2 | async-start | bytes 8388608
  239.2 48.1 %slice-start.1 = ((s8[5242880]{0:T(1024)(128)(4,1)}), s8[1048576]{0:T(1024)(128)(4,1)S(1)}, s32[]{:S(2)}) async-start(s8[5242880]{0:T(1024)(128)(4,1)} %bitcast.108), calls=%async_computation.3 | async-start | bytes 2097152
  239.2 48.1 %copy-start = (f32[5,128,1,2048]{3,1,2,0:T(8,128)S(1)}, f32[5,128,1,2048]{3,1,2,0:T(8,128)}, u32[]{:S(2)}) copy-start(f32[5,128,1,2048]{3,1,2,0:T(8,128)} %copy.73) | copy-start | bytes 15728644
  241.0 46.3 %collective-permute-start.5 = (f32[128,2,2048]{2,0,1:T(8,128)S(1)}, f32[128,2,2048]{2,0,1:T(8,128)S(1)}, u32[]{:S(2)}, u32[]{:S(2)}) collective-permute-start(f32[128,2,2048]{2,0,1:T(8,128)S(1)} %fusion.25), channel_id=1, source_target_pairs={{4,0},{8,4},{12,8},{16,12},{20,16},{24,20},{28,24},{5,1},{9,5},{13... | collective-permute-start | bytes 6291464 | tf_op jit(solution)/shard_map/ppermute | solution.py:15
  287.7 45.6 %collective-permute-start.6 = (f32[128,2,2048]{2,0,1:T(8,128)S(1)}, f32[128,2,2048]{2,0,1:T(8,128)S(1)}, u32[]{:S(2)}, u32[]{:S(2)}) collective-permute-start(f32[128,2,2048]{2,0,1:T(8,128)S(1)} %fusion.28), channel_id=1, source_target_pairs={{4,0},{8,4},{12,8},{16,12},{20,16},{24,20},{28,24},{5,1},{9,5},{13... | collective-permute-start | bytes 6291464 | tf_op jit(solution)/shard_map/ppermute | solution.py:15
  333.6 47.3 %copy-start.2 = (bf16[640,1,2048]{0,2,1:T(8,128)(2,1)S(1)}, bf16[640,1,2048]{0,2,1:T(8,128)(2,1)}, u32[]{:S(2)}) copy-start(bf16[640,1,2048]{0,2,1:T(8,128)(2,1)} %copy.62) | copy-start | bytes 7864324
  333.6 47.3 %copy-start.3 = (bf16[16,128,640]{2,1,0:T(8,128)(2,1)S(1)}, bf16[16,128,640]{2,1,0:T(8,128)(2,1)}, u32[]{:S(2)}) copy-start(bf16[16,128,640]{2,1,0:T(8,128)(2,1)} %fusion.2) | copy-start | bytes 7864324
  333.6 44.4 %collective-permute-start.7 = (f32[128,2,2048]{2,0,1:T(8,128)S(1)}, f32[128,2,2048]{2,0,1:T(8,128)S(1)}, u32[]{:S(2)}, u32[]{:S(2)}) collective-permute-start(f32[128,2,2048]{2,0,1:T(8,128)S(1)} %fusion.31), channel_id=1, source_target_pairs={{4,0},{8,4},{12,8},{16,12},{20,16},{24,20},{28,24},{5,1},{9,5},{13... | collective-permute-start | bytes 6291464 | tf_op jit(solution)/shard_map/ppermute | solution.py:15
  379.6 43.3 %collective-permute-start.8 = (f32[128,2,2048]{2,0,1:T(8,128)}, f32[128,2,2048]{2,0,1:T(8,128)}, u32[]{:S(2)}, u32[]{:S(2)}) collective-permute-start(f32[128,2,2048]{2,0,1:T(8,128)} %fusion.23), channel_id=1, source_target_pairs={{4,0},{8,4},{12,8},{16,12},{20,16},{24,20},{28,24},{5,1},{9,5},{13... | collective-permute-start | bytes 6291464 | tf_op jit(solution)/shard_map/ppermute | solution.py:15
  385.5 39.9 %copy-start.1 = (f32[128,1,2048]{2,0,1:T(8,128)S(1)}, f32[128,1,2048]{2,0,1:T(8,128)}, u32[]{:S(2)}) copy-start(f32[128,1,2048]{2,0,1:T(8,128)} %copy.75) | copy-start | bytes 3145732
  429.0 8.3 %collective-permute-start.9 = (f32[6,3,2048]{2,0,1:T(8,128)S(1)}, f32[6,3,2048]{2,0,1:T(8,128)S(1)}, u32[]{:S(2)}, u32[]{:S(2)}) collective-permute-start(f32[6,3,2048]{2,0,1:T(8,128)S(1)} %fusion.45), channel_id=1, source_target_pairs={{4,0},{8,4},{12,8},{16,12},{20,16},{24,20},{28,24},{5,1},{9,5},{13... | collective-permute-start | bytes 442376 | tf_op jit(solution)/shard_map/ppermute | solution.py:15
  430.4 0.7 copy-start.10
  431.1 6.6 %copy-start.13 = (f32[3,1,2048]{2,0,1:T(4,128)S(1)}, f32[3,1,2048]{2,0,1:T(4,128)}, u32[]{:S(2)}) copy-start(f32[3,1,2048]{2,0,1:T(4,128)} %copy-done.12) | copy-start | bytes 73732
  440.3 6.5 %copy-start.11 = (f32[3,7,2048]{2,0,1:T(4,128)S(1)}, f32[3,7,2048]{2,0,1:T(4,128)}, u32[]{:S(2)}) copy-start(f32[3,7,2048]{2,0,1:T(4,128)} %copy-done.10) | copy-start | bytes 516100
  440.4 6.5 %copy-start.16 = (f32[3,2048]{1,0:T(4,128)S(1)}, f32[3,2048]{1,0:T(4,128)}, u32[]{:S(2)}) copy-start(f32[3,2048]{1,0:T(4,128)} %get-tuple-element.16) | copy-start | bytes 73732
  440.4 6.5 %copy-start.15 = (f32[3,2048]{1,0:T(4,128)S(1)}, f32[3,2048]{1,0:T(4,128)}, u32[]{:S(2)}) copy-start(f32[3,2048]{1,0:T(4,128)} %get-tuple-element.15) | copy-start | bytes 73732
  443.1 23.3 %copy-start.8 = (bf16[128,16,128]{0,2,1:T(8,128)(2,1)S(1)}, bf16[128,16,128]{0,2,1:T(8,128)(2,1)}, u32[]{:S(2)}) copy-start(bf16[128,16,128]{0,2,1:T(8,128)(2,1)} %get-tuple-element.41) | copy-start | bytes 1572868
  443.1 33.8 %all-to-all-start.1 = ((bf16[128,3,2048]{2,1,0:T(4,128)(2,1)}), bf16[128,3,2048]{2,1,0:T(4,128)(2,1)S(1)}, u32[]{:S(2)}, u32[]{:S(2)}) async-start(bf16[128,3,2048]{2,1,0:T(4,128)(2,1)} %copy.76), calls=%async_computation.1 | async-start | bytes 4194304 | tf_op jit(solution)/shard_map/all_to_all | solution.py:119
  446.9 9.2 %collective-permute-start.10 = (f32[3,7,2048]{2,0,1:T(4,128)S(1)}, f32[3,7,2048]{2,0,1:T(4,128)S(1)}, u32[]{:S(2)}, u32[]{:S(2)}) collective-permute-start(f32[3,7,2048]{2,0,1:T(4,128)S(1)} %bitcast_dynamic-update-slice_fusion), channel_id=1, source_target_pairs={{0,4},{4,0},{8,12},{12,8},{16,20},{20,16},{24,28},{28,24},{1,5},{5... | collective-permute-start | bytes 516104 | tf_op jit(solution)/shard_map/ppermute | solution.py:116
  456.1 7.4 %collective-permute-start.11 = (f32[3,7,2048]{2,0,1:T(4,128)S(1)}, f32[3,7,2048]{2,0,1:T(4,128)S(1)}, u32[]{:S(2)}, u32[]{:S(2)}) collective-permute-start(f32[3,7,2048]{2,0,1:T(4,128)S(1)} %add.139), channel_id=1, source_target_pairs={{0,8},{4,12},{8,0},{12,4},{16,24},{20,28},{24,16},{28,20},{1,9},{5... | collective-permute-start | bytes 516104 | tf_op jit(solution)/shard_map/ppermute | solution.py:116
  463.7 12.4 %collective-permute-start.12 = (f32[3,7,2048]{2,0,1:T(4,128)S(1)}, f32[3,7,2048]{2,0,1:T(4,128)S(1)}, u32[]{:S(2)}, u32[]{:S(2)}) collective-permute-start(f32[3,7,2048]{2,0,1:T(4,128)S(1)} %add.140), channel_id=1, source_target_pairs={{0,16},{4,20},{8,24},{12,28},{16,0},{20,4},{24,8},{28,12},{1,17},{... | collective-permute-start | bytes 516104 | tf_op jit(solution)/shard_map/ppermute | solution.py:116
